TPU v7x, 32 devices: a whole 2x2x4 slice. The times are simulated.
32 devices in a mesh: seq: 8 (over y, x, core), ch: 4 (over z).
Axes of the slice: x: 2, y: 2, z: 4, core: 2. Of those that a mesh axis runs over, the one named last changes fastest.
Arguments:
- out_gate: bfloat16 [4096, 1024], P('ch', 'seq'), may hold values from -6 to 6
- key_proj: bfloat16 [4096, 1024], P('ch', 'seq'), may hold values from -6 to 6
- value_proj: bfloat16 [4096, 1024], P('ch', 'seq'), may hold values from -6 to 6
- long_filter: bfloat16 [4096, 1024], P('ch', 'seq'), may hold values from -0.1875 to 0.1875
- skip_gain: float32 [4096], P('ch'), may hold values from -4 to 4
- residual: bfloat16 [4096, 1024], P('ch', 'seq'), may hold values from -6 to 6
- norm_gain: float32 [4096], P('ch'), may hold values from 0.5 to 1.5
Outputs:
- mixed: bfloat16 [4096, 1024], P('ch', 'seq')
- normed: bfloat16 [4096, 1024], P('ch', 'seq')
All inputs are finite; a program needn't handle non-finite values.
Results may differ from a plain program's by a relative error of at most 0.0075.
Values may be sent and summed in bfloat16 or wider, within the bound.
A program may use at most 64 MiB of HBM per device.

v0:
```python
import math

import jax
import jax.numpy as jnp
from jax import lax
from jax.sharding import PartitionSpec as P

D = 4096


HIGHEST = lax.Precision.HIGHEST


def tables(count, span, period):
    row_ids = jnp.arange(count, dtype=jnp.int32)[:, None]
    col_ids = jnp.arange(span, dtype=jnp.int32)[None, :]
    phases = (row_ids * col_ids % period).astype(jnp.float32) * (2.0 * math.pi / period)
    return (jnp.cos(phases), jnp.sin(phases))


def product(left, right):
    return jnp.dot(left, right, precision=HIGHEST, preferred_element_type=jnp.float32)


def block_spectrum(signal):
    width = signal.shape[1]
    cosine, sine = tables(width, 2 * width, 2 * width)
    return (product(signal, cosine), -product(signal, sine))


def block_inverse(real_part, imag_part):
    span = real_part.shape[1]
    cosine, sine = tables(span, span, span)
    return (product(real_part, cosine) - product(imag_part, sine)) / span


def index_convolve(input_real, input_imag, filter_real, filter_imag):
    blocks = input_real.shape[0]
    forward_cos, forward_sin = tables(2 * blocks, blocks, 2 * blocks)

    def forward(real_part, imag_part):
        return (
            product(forward_cos, real_part) + product(forward_sin, imag_part),
            product(forward_cos, imag_part) - product(forward_sin, real_part),
        )

    signal_real, signal_imag = forward(input_real, input_imag)
    kernel_real, kernel_imag = forward(filter_real, filter_imag)
    joint_real = signal_real * kernel_real - signal_imag * kernel_imag
    joint_imag = signal_real * kernel_imag + signal_imag * kernel_real
    back_cos, back_sin = tables(blocks, 2 * blocks, 2 * blocks)
    result_real = (product(back_cos, joint_real) - product(back_sin, joint_imag)) / (2 * blocks)
    result_imag = (product(back_cos, joint_imag) + product(back_sin, joint_real)) / (2 * blocks)
    return (result_real, result_imag)


def on_device(out_gate, key_proj, value_proj, long_filter, skip_gain, residual, norm_gain):
    chans, width = key_proj.shape
    blocks = lax.axis_size("seq")
    product_in = (key_proj.astype(jnp.float32) * value_proj.astype(jnp.float32)).astype(
        jnp.bfloat16
    )
    signal_f = product_in.astype(jnp.float32)
    whole_in, whole_filter = (
        lax.all_to_all(product_in, "seq", split_axis=0, concat_axis=1, tiled=True),
        lax.all_to_all(long_filter, "seq", split_axis=0, concat_axis=1, tiled=True),
    )
    group = whole_in.shape[0]

    def by_block(array):
        return (
            array.astype(jnp.float32)
            .reshape(group, blocks, width)
            .transpose(1, 0, 2)
            .reshape(blocks * group, width)
        )

    signal_real, signal_imag = block_spectrum(by_block(whole_in))
    kernel_real, kernel_imag = block_spectrum(by_block(whole_filter))
    result_real, result_imag = index_convolve(
        signal_real.reshape(blocks, -1),
        signal_imag.reshape(blocks, -1),
        kernel_real.reshape(blocks, -1),
        kernel_imag.reshape(blocks, -1),
    )
    timeline = block_inverse(
        result_real.reshape(blocks * group, 2 * width),
        result_imag.reshape(blocks * group, 2 * width),
    ).reshape(blocks, group, 2 * width)
    upper = timeline[:, :, width:]
    carried = jnp.concatenate([jnp.zeros((1, group, width), jnp.float32), upper[:-1]], axis=0)
    whole_out = (timeline[:, :, :width] + carried).transpose(1, 0, 2).reshape(group, blocks * width)
    convolved = lax.all_to_all(whole_out, "seq", split_axis=1, concat_axis=0, tiled=True)
    total = residual.astype(jnp.float32) + out_gate.astype(jnp.float32) * (
        convolved + skip_gain[:, None] * signal_f
    )
    squares = lax.psum(jnp.sum(total * total, axis=0), "ch")
    normed = total * lax.rsqrt(squares / D + 1e-06)[None, :] * norm_gain[:, None]
    return (total.astype(jnp.bfloat16), normed.astype(jnp.bfloat16))


def solution(mesh):
    return jax.shard_map(
        on_device,
        mesh=mesh,
        in_specs=(
            P("ch", "seq"),
            P("ch", "seq"),
            P("ch", "seq"),
            P("ch", "seq"),
            P("ch"),
            P("ch", "seq"),
            P("ch"),
        ),
        out_specs=(P("ch", "seq"), P("ch", "seq")),
        check_vma=False,
    )
```

profile of v0, /device:TPU:0, one launch (start us, length us, event | category | flops | bytes accessed | tf_op | source)
XLA Modules:
  0.0 86.7 jit_solution(10550059197464009538)
XLA Ops:
  1.7 11.9 %all_to_all.42 = bf16[8,128,128]{2,1,0:T(8,128)(2,1)S(1)} all-to-all(bf16[8,128,128]{2,1,0:T(8,128)(2,1)S(1)} %bitcast.44), channel_id=1, replica_groups=mesh['seq'=8,'ch'=4] {'seq'}, dimensions={0} | all-to-all | bytes 524288 | tf_op jit(solution)/shard_map/all_to_all | solution.py:65
  13.6 3.4 %all-to-all-start.1 = ((bf16[8,128,128]{2,1,0:T(8,128)(2,1)}), bf16[8,128,128]{2,1,0:T(8,128)(2,1)S(1)}, u32[]{:S(2)}, u32[]{:S(2)}) async-start(bf16[8,128,128]{2,1,0:T(8,128)(2,1)} %bitcast.45), calls=%async_computation.1 | async-start | bytes 524288 | tf_op jit(solution)/shard_map/all_to_all | solution.py:66
  19.2 4.7 %all-to-all-done.1 = bf16[8,128,128]{2,1,0:T(8,128)(2,1)S(1)} async-done(((bf16[8,128,128]{2,1,0:T(8,128)(2,1)}), bf16[8,128,128]{2,1,0:T(8,128)(2,1)S(1)}, u32[]{:S(2)}, u32[]{:S(2)}) %all-to-all-start.1) | async-done | bytes 262176 | tf_op jit(solution)/shard_map/all_to_all | solution.py:66
  23.9 2.1 %fusion.2 = f32[1024,256]{0,1:T(8,128)} fusion(bf16[1024,128]{1,0:T(8,128)(2,1)S(1)} %bitcast.40), kind=kOutput, calls=%fused_computation.11 | convolution fusion | flops 403374080 | bytes 1310720 | tf_op jit(solution)/shard_map/dot_general | solution.py:22
  26.0 2.1 %convolution_bitcast_fusion = f32[1024,256]{0,1:T(8,128)} fusion(bf16[1024,128]{1,0:T(8,128)(2,1)S(1)} %bitcast.41), kind=kOutput, calls=%fused_computation.12 | convolution fusion | flops 403111936 | bytes 1310720 | tf_op jit(solution)/shard_map/dot_general | solution.py:22
  28.3 1.2 %reshape.50 = f32[8,32768]{1,0:T(8,128)} reshape(f32[1024,256]{1,0:T(8,128)S(1)} %fusion.27) | data formatting | bytes 2097152 | tf_op jit(solution)/shard_map/reshape | solution.py:81
  29.4 2.6 %copy.10 = f32[1024,256]{1,0:T(8,128)} copy(f32[1024,256]{0,1:T(8,128)} %fusion.2) | data formatting | bytes 2097152 | tf_op jit(solution)/shard_map/neg | solution.py:28
  32.1 1.4 %reshape.54 = f32[8,32768]{1,0:T(8,128)S(1)} reshape(f32[1024,256]{1,0:T(8,128)} %copy.10) | data formatting | bytes 2097152 | tf_op jit(solution)/shard_map/reshape | solution.py:84
  33.5 1.4 %copy.9 = f32[1024,256]{1,0:T(8,128)} copy(f32[1024,256]{0,1:T(8,128)S(1)} %copy-done.1) | data formatting | bytes 2097152 | tf_op jit(solution)/shard_map/dot_general | solution.py:22
  34.8 1.4 %reshape.53 = f32[8,32768]{1,0:T(8,128)S(1)} reshape(f32[1024,256]{1,0:T(8,128)} %copy.9) | data formatting | bytes 2097152 | tf_op jit(solution)/shard_map/reshape | solution.py:83
  36.3 1.8 %fusion.46 = f32[16,32768]{1,0:T(8,128)S(1)} fusion(f32[8,32768]{1,0:T(8,128)S(1)} %reshape.53), kind=kOutput, calls=%fused_computation.67 | convolution fusion | flops 50333440 | bytes 3145728 | tf_op jit(solution)/shard_map/dot_general | solution.py:22
  38.1 1.8 %fusion.42 = f32[16,32768]{1,0:T(8,128)S(1)} fusion(f32[8,32768]{1,0:T(8,128)S(1)} %reshape.54), kind=kOutput, calls=%fused_computation.65 | convolution fusion | flops 50333440 | bytes 3145728 | tf_op jit(solution)/shard_map/dot_general | solution.py:22
  39.9 1.9 %convolution_add_fusion = f32[16,32768]{1,0:T(8,128)S(1)} fusion(f32[16,32768]{1,0:T(8,128)S(1)} %fusion.46, f32[8,32768]{1,0:T(8,128)S(1)} %reshape.54), kind=kOutput, calls=%fused_computation.2 | convolution fusion | flops 50857728 | bytes 5242880 | tf_op jit(solution)/shard_map/dot_general | solution.py:22
  41.8 2.1 %convolution_subtract_fusion = f32[16,32768]{1,0:T(8,128)S(1)} fusion(f32[16,32768]{1,0:T(8,128)S(1)} %fusion.42, f32[8,32768]{1,0:T(8,128)S(1)} %reshape.53), kind=kOutput, calls=%fused_computation | convolution fusion | flops 50857728 | bytes 5242880 | tf_op jit(solution)/shard_map/dot_general | solution.py:22
  43.9 1.8 %fusion.48 = f32[16,32768]{1,0:T(8,128)S(1)} fusion(f32[8,32768]{1,0:T(8,128)S(1)} %copy-done), kind=kOutput, calls=%fused_computation.68 | convolution fusion | flops 50333440 | bytes 3145728 | tf_op jit(solution)/shard_map/dot_general | solution.py:22
  45.8 1.8 %fusion.44 = f32[16,32768]{1,0:T(8,128)S(1)} fusion(f32[8,32768]{1,0:T(8,128)S(1)} %reshape.51), kind=kOutput, calls=%fused_computation.66 | convolution fusion | flops 50333440 | bytes 3145728 | tf_op jit(solution)/shard_map/dot_general | solution.py:22
  47.6 1.9 %convolution_add_fusion.1 = f32[16,32768]{1,0:T(8,128)S(1)} fusion(f32[16,32768]{1,0:T(8,128)S(1)} %fusion.48, f32[8,32768]{1,0:T(8,128)S(1)} %reshape.51), kind=kOutput, calls=%fused_computation.3 | convolution fusion | flops 50857728 | bytes 5242880 | tf_op jit(solution)/shard_map/dot_general | solution.py:22
  49.5 2.4 %multiply_add_fusion = (f32[16,32768]{1,0:T(8,128)S(1)}, f32[16,32768]{1,0:T(8,128)S(1)}) fusion(f32[16,32768]{1,0:T(8,128)S(1)} %convolution_add_fusion, f32[16,32768]{1,0:T(8,128)S(1)} %convolution_add_fusion.1, f32[16,32768]{1,0:T(8,128)S(1)} %convolution_subtract_fusion, f32[16,32768]{1,0:T(8,128)S(1)} %fusion.44, f32[8,32768]{1,0:T(8,128)S(1)} %copy-done), kind=kOutput, calls=%fused_computation.8 | convolution fusion | flops 54003456 | bytes 13631488 | tf_op jit(solution)/shard_map/dot_general | solution.py:22
  54.2 1.1 %fusion = f32[8,32768]{1,0:T(8,128)S(1)} fusion(f32[8,32768]{1,0:T(8,128)S(1)} %fusion.59, f32[16,32768]{1,0:T(8,128)S(1)} %get-tuple-element.5), kind=kOutput, calls=%fused_computation.5 | convolution fusion | flops 50857728 | bytes 4194304 | tf_op jit(solution)/shard_map/dot_general | solution.py:22
  55.4 1.1 %fusion.1 = f32[8,32768]{1,0:T(8,128)S(1)} fusion(f32[8,32768]{1,0:T(8,128)S(1)} %fusion.61, f32[16,32768]{1,0:T(8,128)S(1)} %get-tuple-element.4), kind=kOutput, calls=%fused_computation.7 | convolution fusion | flops 50857728 | bytes 4194304 | tf_op jit(solution)/shard_map/dot_general | solution.py:22
  56.7 2.2 %fusion.11 = f32[1024,256]{1,0:T(8,128)S(1)} fusion(f32[1024,256]{1,0:T(8,128)S(1)} %reshape.55), kind=kOutput, calls=%fused_computation.31 | convolution fusion | flops 806223872 | bytes 2097152 | tf_op jit(solution)/shard_map/dot_general | solution.py:22
  59.1 2.0 %fusion.3 = f32[1024,256]{1,0:T(8,128)S(1)} fusion(f32[1024,256]{1,0:T(8,128)S(1)} %fusion.11, f32[1024,256]{1,0:T(8,128)S(1)} %reshape.56), kind=kOutput, calls=%fused_computation.15 | convolution fusion | flops 806748160 | bytes 3145728 | tf_op jit(solution)/shard_map/dot_general | solution.py:22
  61.2 12.3 %all_to_all.43 = f32[128,8,128]{2,0,1:T(8,128)S(1)} all-to-all(f32[128,8,128]{2,0,1:T(8,128)S(1)} %fusion.4), channel_id=1, replica_groups=mesh['seq'=8,'ch'=4] {'seq'}, dimensions={1} | all-to-all | bytes 1048576 | tf_op jit(solution)/shard_map/all_to_all | solution.py:93
  73.7 12.0 %psum.7 = f32[128]{0:T(128)S(1)} all-reduce(f32[128]{0:T(128)S(1)} %get-tuple-element.2), channel_id=1, replica_groups=mesh['seq'=8,'ch'=4] {'ch'}, use_global_device_ids=true, to_apply=%region_1.2 | all-reduce | flops 128 | bytes 1024 | tf_op jit(solution)/shard_map/psum | solution.py:97
  (25 shorter events, 7.4 us)
Async XLA Ops:
  13.6 10.3 %all-to-all-start.1 = ((bf16[8,128,128]{2,1,0:T(8,128)(2,1)}), bf16[8,128,128]{2,1,0:T(8,128)(2,1)S(1)}, u32[]{:S(2)}, u32[]{:S(2)}) async-start(bf16[8,128,128]{2,1,0:T(8,128)(2,1)} %bitcast.45), calls=%async_computation.1 | async-start | bytes 524288 | tf_op jit(solution)/shard_map/all_to_all | solution.py:66
  29.4 4.0 %copy-start.1 = (f32[1024,256]{0,1:T(8,128)S(1)}, f32[1024,256]{0,1:T(8,128)}, u32[]{:S(2)}) copy-start(f32[1024,256]{0,1:T(8,128)} %convolution_bitcast_fusion) | copy-start | bytes 3145732
  41.8 2.1 %copy-start = (f32[8,32768]{1,0:T(8,128)S(1)}, f32[8,32768]{1,0:T(8,128)}, u32[]{:S(2)}) copy-start(f32[8,32768]{1,0:T(8,128)} %reshape.50) | copy-start | bytes 3145732
  61.0 12.4 %copy-start.2 = (bf16[1024,128]{1,0:T(8,128)(2,1)S(1)}, bf16[1024,128]{1,0:T(8,128)(2,1)}, u32[]{:S(2)}) copy-start(bf16[1024,128]{1,0:T(8,128)(2,1)} %param.7) | copy-start | bytes 786436
  61.1 12.4 %copy-start.3 = (bf16[1024,128]{1,0:T(8,128)(2,1)S(1)}, bf16[1024,128]{1,0:T(8,128)(2,1)}, u32[]{:S(2)}) copy-start(bf16[1024,128]{1,0:T(8,128)(2,1)} %param.12) | copy-start | bytes 786436
  61.1 12.4 %copy-start.4 = (f32[1024]{0:T(1024)S(1)}, f32[1024]{0:T(1024)}, u32[]{:S(2)}) copy-start(f32[1024]{0:T(1024)} %param.11) | copy-start | bytes 12292
  61.1 24.6 %copy-start.5 = (f32[1024]{0:T(1024)S(1)}, f32[1024]{0:T(1024)}, u32[]{:S(2)}) copy-start(f32[1024]{0:T(1024)} %param.13) | copy-start | bytes 12292
where the time goes:
time: 87.1 us; the launch traced here: 86.7 us
  blocking collectives  36.1 us (41%)
  matrix products  30.6 us (35%)
  local copies, waits for them, and re-layouts  8.56 us (10%)
  waiting for transfers between devices  4.67 us (5%)
  starting transfers between devices  3.41 us (4%)
  other arithmetic  2.43 us (3%)
    dot_general x18, matrix products, product(): jnp.dot(left, right, precision=HIGHEST, preferred_element_type=jnp.float32)  30.6 us
    all_to_all x1, blocking collectives, on_device(): lax.all_to_all(whole_out, 'seq', split_axis=1, concat_axis=0, tiled=True)  12.3 us
    psum x1, blocking collectives, on_device(): squares = lax.psum(jnp.sum(total * total, axis=0), 'ch')  12 us
    all_to_all x1, blocking collectives, on_device(): lax.all_to_all(product_in, 'seq', split_axis=0, concat_axis=1, tiled=True)  11.9 us
    all_to_all x1, waiting for transfers between devices, on_device(): lax.all_to_all(long_filter, 'seq', split_axis=0, concat_axis=1, tiled=True)  4.67 us
    all_to_all x1, starting transfers between devices, on_device(): lax.all_to_all(long_filter, 'seq', split_axis=0, concat_axis=1, tiled=True)  3.41 us
    neg x1, local copies, waits for them, and re-layouts, block_spectrum(): return (product(signal, cosine), -product(signal, sine))  2.63 us
  transfers between devices with their start and end apart: 1, of which 1 were waited for; matrix products, arithmetic and copies ran while one was open for 2% of the time, Pallas kernels for 0%

commit v1 on v0

--- a/solution.py
+++ b/solution.py
@@ -1,8 +1,12 @@
 import math
+
+import numpy as np
 
 import jax
 import jax.numpy as jnp
 from jax import lax
+from jax.experimental import pallas as pl
+from jax.experimental.pallas import tpu as pltpu
 from jax.sharding import PartitionSpec as P
 
 D = 4096
@@ -99,9 +103,265 @@
     return (total.astype(jnp.bfloat16), normed.astype(jnp.bfloat16))
 
 
+CHUNKS = 2
+
+
+def spectral_tables(width):
+    n = np.arange(width)[:, None]
+    k = np.arange(width)[None, :]
+    angle = 2.0 * np.pi * (2 * k + 1) * n / (4 * width)
+    forward = np.concatenate([np.cos(angle), -np.sin(angle)], axis=1)
+    inverse = forward.T / width
+
+    def split(table):
+        high = table.astype(jnp.bfloat16)
+        low = (table - high.astype(np.float64)).astype(jnp.bfloat16)
+        return high, low
+
+    return (
+        np.concatenate(split(forward), axis=0),
+        np.concatenate(split(inverse), axis=1),
+    )
+
+
+def fused(
+    key_hbm, value_hbm, filter_hbm, gate_hbm, residual_hbm, skip_ref, gain_ref, forward_ref, inverse_ref,
+    mixed_ref, normed_ref,
+    key_v, value_v, gate_v, residual_v, product_v, signal_in, filter_in, signal_spec, filter_spec, joint,
+    back_out, back_in, total_v, squares_v, load_sem, send_sem, recv_sem, back_send, back_recv, sq_send, sq_recv,
+):
+    blocks, group, width = key_hbm.shape
+    me = lax.axis_index("seq")
+    lane = lax.axis_index("ch")
+    lanes = squares_v.shape[0]
+    rows = group // CHUNKS
+
+    loads = [
+        pltpu.make_async_copy(source, target, load_sem.at[i])
+        for i, (source, target) in enumerate(
+            ((key_hbm, key_v), (value_hbm, value_v), (filter_hbm.at[me], filter_in.at[me]),
+             (gate_hbm, gate_v), (residual_hbm, residual_v))
+        )
+    ]
+    for load in loads:
+        load.start()
+    barrier = pltpu.get_barrier_semaphore()
+    for step in range(1, lanes):
+        pl.semaphore_signal(barrier, inc=1, device_id={"ch": lax.rem(lane + step, lanes)})
+    for step in range(1, blocks):
+        pl.semaphore_signal(barrier, inc=1, device_id={"seq": lax.rem(me + step, blocks)})
+    loads[0].wait()
+    loads[1].wait()
+    product_v[...] = (key_v[...].astype(jnp.float32) * value_v[...].astype(jnp.float32)).astype(jnp.bfloat16)
+    pl.semaphore_wait(barrier, blocks - 1 + lanes - 1)
+
+    def outbound(kind, chunk, step):
+        peer = lax.rem(me + step, blocks)
+        source, target = ((filter_hbm, filter_in), (product_v, signal_in))[kind]
+        span = pl.ds(chunk * rows, rows)
+        return pltpu.make_async_remote_copy(
+            src_ref=source.at[peer, span],
+            dst_ref=target.at[me, span],
+            send_sem=send_sem.at[kind, chunk, step],
+            recv_sem=recv_sem.at[kind, chunk, step],
+            device_id={"seq": peer},
+        )
+
+    def inbound(kind, chunk, step):
+        origin = lax.rem(me + blocks - step, blocks)
+        target = (filter_in, signal_in)[kind]
+        span = pl.ds(chunk * rows, rows)
+        return pltpu.make_async_remote_copy(
+            src_ref=target.at[origin, span],
+            dst_ref=target.at[origin, span],
+            send_sem=send_sem.at[kind, chunk, step],
+            recv_sem=recv_sem.at[kind, chunk, step],
+            device_id={"seq": origin},
+        )
+
+    def returning(chunk, step):
+        peer = lax.rem(me + step, blocks)
+        span = pl.ds(chunk * rows, rows)
+        return pltpu.make_async_remote_copy(
+            src_ref=back_out.at[peer, span],
+            dst_ref=back_in.at[me, span],
+            send_sem=back_send.at[chunk, step],
+            recv_sem=back_recv.at[chunk, step],
+            device_id={"seq": peer},
+        )
+
+    def returned(chunk, step):
+        origin = lax.rem(me + blocks - step, blocks)
+        span = pl.ds(chunk * rows, rows)
+        return pltpu.make_async_remote_copy(
+            src_ref=back_in.at[origin, span],
+            dst_ref=back_in.at[origin, span],
+            send_sem=back_send.at[chunk, step],
+            recv_sem=back_recv.at[chunk, step],
+            device_id={"seq": origin},
+        )
+
+    for chunk in range(CHUNKS):
+        for kind in range(2):
+            for step in range(1, blocks):
+                outbound(kind, chunk, step).start()
+
+    signal_in[me] = product_v[me]
+    loads[2].wait()
+    loads[3].wait()
+    loads[4].wait()
+    for b in range(blocks):
+        skip = jnp.transpose(jnp.broadcast_to(skip_ref[b : b + 1, :], (width, group)))
+        total_v[b] = residual_v[b].astype(jnp.float32) + gate_v[b].astype(jnp.float32) * (
+            skip * product_v[b].astype(jnp.float32)
+        )
+
+    sign = (1 - 2 * (lax.broadcasted_iota(jnp.int32, (8, width), 1) % 2)).astype(jnp.float32)
+
+    def spectrum(ref, chunk, out_ref):
+        part = ref[:, chunk * rows : (chunk + 1) * rows, :].reshape(blocks * rows, width)
+        doubled = jnp.concatenate([part, part], axis=1)
+        out_ref[...] = jnp.dot(doubled, forward_ref[...], preferred_element_type=jnp.float32).reshape(
+            blocks, rows, 2 * width
+        )
+
+    for chunk in range(CHUNKS):
+        for step in range(1, blocks):
+            inbound(0, chunk, step).wait_recv()
+        spectrum(filter_in, chunk, filter_spec)
+        for step in range(1, blocks):
+            inbound(1, chunk, step).wait_recv()
+        spectrum(signal_in, chunk, signal_spec)
+
+        def one_octet(octet, carry):
+            span = pl.ds(pl.multiple_of(octet * 8, 8), 8)
+            plain_r = [signal_spec[b, span, :width] for b in range(blocks)]
+            plain_i = [signal_spec[b, span, width:] for b in range(blocks)]
+            input_r, input_i = [plain_r[0]], [plain_i[0]]
+            for b in range(1, blocks):
+                input_r.append(plain_r[b] - sign * plain_i[b - 1])
+                input_i.append(plain_i[b] + sign * plain_r[b - 1])
+            taps_r = [filter_spec[b, span, :width] for b in range(blocks)]
+            taps_i = [filter_spec[b, span, width:] for b in range(blocks)]
+            for j in range(blocks):
+                real = taps_r[0] * input_r[j] - taps_i[0] * input_i[j]
+                imag = taps_r[0] * input_i[j] + taps_i[0] * input_r[j]
+                for d in range(1, j + 1):
+                    real = real + taps_r[d] * input_r[j - d] - taps_i[d] * input_i[j - d]
+                    imag = imag + taps_r[d] * input_i[j - d] + taps_i[d] * input_r[j - d]
+                joint[j, span, :width] = real
+                joint[j, span, width:] = imag
+            return carry
+
+        lax.fori_loop(0, rows // 8, one_octet, 0)
+        timeline = jnp.dot(
+            joint[...].reshape(blocks * rows, 2 * width).astype(jnp.bfloat16),
+            inverse_ref[...],
+            preferred_element_type=jnp.float32,
+        )
+        timeline = (timeline[:, :width] + timeline[:, width:]).astype(jnp.bfloat16)
+        back_out[:, chunk * rows : (chunk + 1) * rows, :] = timeline.reshape(blocks, rows, width)
+        for step in range(1, blocks):
+            returning(chunk, step).start()
+    back_in[me] = back_out[me]
+
+    squares = jnp.zeros((8, width), jnp.float32)
+    for chunk in range(CHUNKS):
+        for step in range(1, blocks):
+            returned(chunk, step).wait_recv()
+        for b in range(blocks):
+            span = pl.ds(chunk * rows, rows)
+            total = total_v[b, span] + gate_v[b, span].astype(jnp.float32) * back_in[b, span].astype(jnp.float32)
+            total_v[b, span] = total
+            squares = squares + jnp.sum((total * total).reshape(rows // 8, 8, width), axis=0)
+    squares_v[lane] = squares
+
+    def share(step, other):
+        return pltpu.make_async_remote_copy(
+            src_ref=squares_v.at[other[0]],
+            dst_ref=squares_v.at[other[0]],
+            send_sem=sq_send.at[step],
+            recv_sem=sq_recv.at[step],
+            device_id={"ch": other[1]},
+        )
+
+    for step in range(1, lanes):
+        share(step, (lane, lax.rem(lane + step, lanes))).start()
+    mixed_ref[...] = total_v[...].astype(jnp.bfloat16)
+    for step in range(1, lanes):
+        origin = lax.rem(lane + lanes - step, lanes)
+        share(step, (origin, origin)).wait_recv()
+    everyone = jnp.sum(jnp.sum(squares_v[...], axis=0), axis=0, keepdims=True)
+    scale = lax.rsqrt(everyone / (lanes * blocks * group) + 1e-06)
+    for b in range(blocks):
+        gain = jnp.transpose(jnp.broadcast_to(gain_ref[b : b + 1, :], (width, group)))
+        normed_ref[b] = (total_v[b] * scale * gain).astype(jnp.bfloat16)
+
+    for chunk in range(CHUNKS):
+        for step in range(1, blocks):
+            outbound(0, chunk, step).wait_send()
+            outbound(1, chunk, step).wait_send()
+            returning(chunk, step).wait_send()
+    for step in range(1, lanes):
+        share(step, (lane, lax.rem(lane + step, lanes))).wait_send()
+
+
+def with_kernel(out_gate, key_proj, value_proj, long_filter, skip_gain, residual, norm_gain):
+    chans, width = key_proj.shape
+    blocks, lanes = lax.axis_size("seq"), lax.axis_size("ch")
+    group = chans // blocks
+    rows = group // CHUNKS
+    shape = (blocks, group, width)
+    forward, inverse = spectral_tables(width)
+    bf16, f32 = jnp.bfloat16, jnp.float32
+    anywhere = pl.BlockSpec(memory_space=pl.ANY)
+    local = pl.BlockSpec(memory_space=pltpu.VMEM)
+    dma = pltpu.SemaphoreType.DMA
+    mixed, normed = pl.pallas_call(
+        fused,
+        out_shape=(jax.ShapeDtypeStruct(shape, bf16), jax.ShapeDtypeStruct(shape, bf16)),
+        in_specs=[anywhere] * 5 + [local] * 4,
+        out_specs=(local, local),
+        scratch_shapes=[
+            *[pltpu.VMEM(shape, bf16) for _ in range(7)],
+            *[pltpu.VMEM((blocks, rows, 2 * width), f32) for _ in range(3)],
+            pltpu.VMEM(shape, bf16),
+            pltpu.VMEM(shape, bf16),
+            pltpu.VMEM(shape, f32),
+            pltpu.VMEM((lanes, 8, width), f32),
+            dma((5,)),
+            dma((2, CHUNKS, blocks)),
+            dma((2, CHUNKS, blocks)),
+            dma((CHUNKS, blocks)),
+            dma((CHUNKS, blocks)),
+            dma((lanes,)),
+            dma((lanes,)),
+        ],
+        compiler_params=pltpu.CompilerParams(collective_id=0, has_side_effects=True),
+    )(
+        key_proj.reshape(shape),
+        value_proj.reshape(shape),
+        long_filter.reshape(shape),
+        out_gate.reshape(shape),
+        residual.reshape(shape),
+        skip_gain.reshape(blocks, group),
+        norm_gain.reshape(blocks, group),
+        jnp.asarray(forward),
+        jnp.asarray(inverse),
+    )
+    return mixed.reshape(chans, width), normed.reshape(chans, width)
+
+
+def choose(out_gate, key_proj, *rest):
+    chans, width = key_proj.shape
+    blocks = lax.axis_size("seq")
+    tiled = chans % (blocks * CHUNKS * 16) == 0 and width % 128 == 0 and blocks <= 16
+    return (with_kernel if tiled else on_device)(out_gate, key_proj, *rest)
+
+
 def solution(mesh):
     return jax.shard_map(
-        on_device,
+        choose,
         mesh=mesh,
         in_specs=(
             P("ch", "seq"),

time: 87.1 us -> 27.8 us (0.32)
  blocking collectives: 36.1 us -> 0 us
  matrix products: 30.6 us -> 0 us
  Pallas kernels: 0 us -> 24.6 us
  local copies, waits for them, and re-layouts: 8.56 us -> 2.42 us
  waiting for transfers between devices: 4.67 us -> 0 us
  starting transfers between devices: 3.41 us -> 0 us
  other arithmetic: 2.43 us -> 0 us
    dot_general x18 -> x0, matrix products: 30.6 us -> none  [product(): jnp.dot(left, right, precision=HIGHEST, preferred_element_type=jnp.float32)]
    pallas_call x0 -> x1, Pallas kernels: none -> 24.6 us  [with_kernel(): pl.pallas_call(fused, out_shape=(jax.ShapeDtypeStruct(shape, bf16), jax.S...]
    all_to_all x2 -> x0, blocking collectives: 24.2 us -> none  [the longest x1 12.3 us: on_device(): lax.all_to_all(whole_out, 'seq', split_axis=1, concat_axis=0, tiled=True)]
    psum x1 -> x0, blocking collectives: 12 us -> none  [on_device(): squares = lax.psum(jnp.sum(total * total, axis=0), 'ch')]
    all_to_all x1 -> x0, waiting for transfers between devices: 4.67 us -> none  [on_device(): lax.all_to_all(long_filter, 'seq', split_axis=0, concat_axis=1, tiled=True)]
    reshape x6 -> x0, local copies, waits for them, and re-layouts: 4.51 us -> none  [the longest x1 1.42 us: on_device(): kernel_imag.reshape(blocks, -1)]
    all_to_all x1 -> x0, starting transfers between devices: 3.41 us -> none  [on_device(): lax.all_to_all(long_filter, 'seq', split_axis=0, concat_axis=1, tiled=True)]
    neg x1 -> x0, local copies, waits for them, and re-layouts: 2.63 us -> none  [block_spectrum(): return (product(signal, cosine), -product(signal, sine))]
  transfers between devices with their start and end apart: 1 -> 0, of which waited for: 1 -> 0; matrix products, arithmetic and copies ran while one was open for 2% -> 0% of each run, Pallas kernels for 0% -> 0%
where the time goes in v1:
time: 27.8 us; the launch traced here: 27.6 us
  Pallas kernels  24.6 us (88%)
  local copies, waits for them, and re-layouts  2.42 us (9%)
  between operations  0.65 us (2%)
    pallas_call x1, Pallas kernels, with_kernel(): pl.pallas_call(fused, out_shape=(jax.ShapeDtypeStruct(shape, bf16), jax.S...  24.6 us
    unnamed x4, local copies, waits for them, and re-layouts  2.42 us

profile of v1, /device:TPU:0, one launch (start us, length us, event | category | flops | bytes accessed | tf_op | source)
XLA Modules:
  0.0 27.6 jit_solution(17064467340232447048)
XLA Ops:
  0.6 24.6 %shard_map.104 = (bf16[8,128,128]{2,1,0:T(8,128)(2,1)}, bf16[8,128,128]{2,1,0:T(8,128)(2,1)}) custom-call(bf16[8,128,128]{2,1,0:T(8,128)(2,1)} %bitcast.11, bf16[8,128,128]{2,1,0:T(8,128)(2,1)} %bitcast.12, bf16[8,128,128]{2,1,0:T(8,128)(2,1)} %bitcast.13, bf16[8,128,128]{2,1,0:T(8,128)(2,1)} %bitcast.14, bf16[8,128,128]{2,1,0:T(8,128)(2,1)} %bitcast.15, ...), custom_call_target="tpu_custom_call" | custom-call | tf_op jit(solution)/shard_map/pallas_call | solution.py:320
  25.2 0.0 copy-start
  25.2 1.7 %copy.13 = bf16[1024,128]{1,0:T(8,128)(2,1)} copy(bf16[1024,128]{1,0:T(8,128)(2,1)} %bitcast.10) | data formatting | bytes 524288
  26.9 0.0 copy-done
  26.9 0.7 %copy.14 = bf16[1024,128]{1,0:T(8,128)(2,1)} copy(bf16[1024,128]{1,0:T(8,128)(2,1)S(1)} %bitcast.9) | data formatting | bytes 524288
Async XLA Ops:
  25.2 1.7 %copy-start = (bf16[8,128,128]{2,1,0:T(8,128)(2,1)S(1)}, bf16[8,128,128]{2,1,0:T(8,128)(2,1)}, u32[]{:S(2)}) copy-start(bf16[8,128,128]{2,1,0:T(8,128)(2,1)} %get-tuple-element.5) | copy-start | bytes 786436

commit v2 on v1

--- a/solution.py
+++ b/solution.py
@@ -125,10 +125,10 @@
 
 
 def fused(
-    key_hbm, value_hbm, filter_hbm, gate_hbm, residual_hbm, skip_ref, gain_ref, forward_ref, inverse_ref,
-    mixed_ref, normed_ref,
-    key_v, value_v, gate_v, residual_v, product_v, signal_in, filter_in, signal_spec, filter_spec, joint,
-    back_out, back_in, total_v, squares_v, load_sem, send_sem, recv_sem, back_send, back_recv, sq_send, sq_recv,
+    key_hbm, value_hbm, filter_hbm, gate_hbm, residual_hbm, skip_hbm, gain_hbm, forward_hbm, inverse_hbm,
+    total_v, scale_ref, columns_v,
+    skip_ref, gain_ref, forward_ref, inverse_ref, key_v, value_v, gate_v, residual_v, pair_out, pair_in, spec, joint,
+    back_out, back_in, squares_v, load_sem, send_sem, recv_sem, back_send, back_recv, sq_send, sq_recv,
 ):
     blocks, group, width = key_hbm.shape
     me = lax.axis_index("seq")
@@ -136,46 +136,46 @@
     lanes = squares_v.shape[0]
     rows = group // CHUNKS
 
-    loads = [
-        pltpu.make_async_copy(source, target, load_sem.at[i])
-        for i, (source, target) in enumerate(
-            ((key_hbm, key_v), (value_hbm, value_v), (filter_hbm.at[me], filter_in.at[me]),
-             (gate_hbm, gate_v), (residual_hbm, residual_v))
-        )
-    ]
-    for load in loads:
-        load.start()
     barrier = pltpu.get_barrier_semaphore()
     for step in range(1, lanes):
         pl.semaphore_signal(barrier, inc=1, device_id={"ch": lax.rem(lane + step, lanes)})
     for step in range(1, blocks):
         pl.semaphore_signal(barrier, inc=1, device_id={"seq": lax.rem(me + step, blocks)})
+    loads = [
+        pltpu.make_async_copy(source, target, load_sem.at[i])
+        for i, (source, target) in enumerate(
+            ((key_hbm, key_v), (value_hbm, value_v), (filter_hbm, pair_out.at[:, 0]),
+             (gate_hbm, gate_v), (residual_hbm, residual_v), (skip_hbm, skip_ref), (gain_hbm, gain_ref),
+             (forward_hbm, forward_ref), (inverse_hbm, inverse_ref))
+        )
+    ]
+    for load in loads:
+        load.start()
+    loads[2].wait()
     loads[0].wait()
     loads[1].wait()
-    product_v[...] = (key_v[...].astype(jnp.float32) * value_v[...].astype(jnp.float32)).astype(jnp.bfloat16)
+    pair_out[:, 1] = (key_v[...].astype(jnp.float32) * value_v[...].astype(jnp.float32)).astype(jnp.bfloat16)
     pl.semaphore_wait(barrier, blocks - 1 + lanes - 1)
 
-    def outbound(kind, chunk, step):
+    def outbound(chunk, step):
         peer = lax.rem(me + step, blocks)
-        source, target = ((filter_hbm, filter_in), (product_v, signal_in))[kind]
         span = pl.ds(chunk * rows, rows)
         return pltpu.make_async_remote_copy(
-            src_ref=source.at[peer, span],
-            dst_ref=target.at[me, span],
-            send_sem=send_sem.at[kind, chunk, step],
-            recv_sem=recv_sem.at[kind, chunk, step],
+            src_ref=pair_out.at[peer, :, span],
+            dst_ref=pair_in.at[me, :, span],
+            send_sem=send_sem.at[chunk, step],
+            recv_sem=recv_sem.at[chunk, step],
             device_id={"seq": peer},
         )
 
-    def inbound(kind, chunk, step):
+    def inbound(chunk, step):
         origin = lax.rem(me + blocks - step, blocks)
-        target = (filter_in, signal_in)[kind]
         span = pl.ds(chunk * rows, rows)
         return pltpu.make_async_remote_copy(
-            src_ref=target.at[origin, span],
-            dst_ref=target.at[origin, span],
-            send_sem=send_sem.at[kind, chunk, step],
-            recv_sem=recv_sem.at[kind, chunk, step],
+            src_ref=pair_in.at[origin, :, span],
+            dst_ref=pair_in.at[origin, :, span],
+            send_sem=send_sem.at[chunk, step],
+            recv_sem=recv_sem.at[chunk, step],
             device_id={"seq": origin},
         )
 
@@ -202,47 +202,39 @@
         )
 
     for chunk in range(CHUNKS):
-        for kind in range(2):
-            for step in range(1, blocks):
-                outbound(kind, chunk, step).start()
-
-    signal_in[me] = product_v[me]
-    loads[2].wait()
-    loads[3].wait()
-    loads[4].wait()
+        for step in range(1, blocks):
+            outbound(chunk, step).start()
+
+    pair_in[me] = pair_out[me]
+    for load in loads[3:]:
+        load.wait()
     for b in range(blocks):
+        columns_v[b] = jnp.transpose(jnp.broadcast_to(gain_ref[b : b + 1, :], (width, group)))
         skip = jnp.transpose(jnp.broadcast_to(skip_ref[b : b + 1, :], (width, group)))
         total_v[b] = residual_v[b].astype(jnp.float32) + gate_v[b].astype(jnp.float32) * (
-            skip * product_v[b].astype(jnp.float32)
+            skip * pair_out[b, 1].astype(jnp.float32)
         )
 
     sign = (1 - 2 * (lax.broadcasted_iota(jnp.int32, (8, width), 1) % 2)).astype(jnp.float32)
 
-    def spectrum(ref, chunk, out_ref):
-        part = ref[:, chunk * rows : (chunk + 1) * rows, :].reshape(blocks * rows, width)
-        doubled = jnp.concatenate([part, part], axis=1)
-        out_ref[...] = jnp.dot(doubled, forward_ref[...], preferred_element_type=jnp.float32).reshape(
-            blocks, rows, 2 * width
-        )
-
     for chunk in range(CHUNKS):
         for step in range(1, blocks):
-            inbound(0, chunk, step).wait_recv()
-        spectrum(filter_in, chunk, filter_spec)
-        for step in range(1, blocks):
-            inbound(1, chunk, step).wait_recv()
-        spectrum(signal_in, chunk, signal_spec)
+            inbound(chunk, step).wait_recv()
+        part = pair_in[:, :, chunk * rows : (chunk + 1) * rows, :].reshape(blocks * 2 * rows, width)
+        spec[...] = jnp.dot(
+            jnp.concatenate([part, part], axis=1), forward_ref[...], preferred_element_type=jnp.float32
+        ).reshape(blocks, 2, rows, 2 * width)
 
         def one_octet(octet, carry):
             span = pl.ds(pl.multiple_of(octet * 8, 8), 8)
-            plain_r = [signal_spec[b, span, :width] for b in range(blocks)]
-            plain_i = [signal_spec[b, span, width:] for b in range(blocks)]
+            plain_r = [spec[b, 1, span, :width] for b in range(blocks)]
+            plain_i = [spec[b, 1, span, width:] for b in range(blocks)]
             input_r, input_i = [plain_r[0]], [plain_i[0]]
             for b in range(1, blocks):
                 input_r.append(plain_r[b] - sign * plain_i[b - 1])
                 input_i.append(plain_i[b] + sign * plain_r[b - 1])
-            taps_r = [filter_spec[b, span, :width] for b in range(blocks)]
-            taps_i = [filter_spec[b, span, width:] for b in range(blocks)]
+            taps_r = [spec[b, 0, span, :width] for b in range(blocks)]
+            taps_i = [spec[b, 0, span, width:] for b in range(blocks)]
             for j in range(blocks):
                 real = taps_r[0] * input_r[j] - taps_i[0] * input_i[j]
                 imag = taps_r[0] * input_i[j] + taps_i[0] * input_r[j]
@@ -287,23 +279,32 @@
 
     for step in range(1, lanes):
         share(step, (lane, lax.rem(lane + step, lanes))).start()
-    mixed_ref[...] = total_v[...].astype(jnp.bfloat16)
     for step in range(1, lanes):
         origin = lax.rem(lane + lanes - step, lanes)
         share(step, (origin, origin)).wait_recv()
     everyone = jnp.sum(jnp.sum(squares_v[...], axis=0), axis=0, keepdims=True)
-    scale = lax.rsqrt(everyone / (lanes * blocks * group) + 1e-06)
-    for b in range(blocks):
-        gain = jnp.transpose(jnp.broadcast_to(gain_ref[b : b + 1, :], (width, group)))
-        normed_ref[b] = (total_v[b] * scale * gain).astype(jnp.bfloat16)
+    scale_ref[...] = lax.rsqrt(everyone / (lanes * blocks * group) + 1e-06)
 
     for chunk in range(CHUNKS):
         for step in range(1, blocks):
-            outbound(0, chunk, step).wait_send()
-            outbound(1, chunk, step).wait_send()
+            outbound(chunk, step).wait_send()
             returning(chunk, step).wait_send()
     for step in range(1, lanes):
         share(step, (lane, lax.rem(lane + step, lanes))).wait_send()
+
+
+def finish(total_ref, scale_ref, columns_ref, mixed_hbm, normed_hbm, mixed_v, normed_v, mixed_sem, normed_sem):
+    blocks = total_ref.shape[0]
+    stores = []
+    for b in range(blocks):
+        mixed_v[b] = total_ref[b].astype(jnp.bfloat16)
+        normed_v[b] = (total_ref[b] * scale_ref[...] * columns_ref[b]).astype(jnp.bfloat16)
+        stores.append(pltpu.make_async_copy(mixed_v.at[b], mixed_hbm.at[b], mixed_sem.at[b]))
+        stores.append(pltpu.make_async_copy(normed_v.at[b], normed_hbm.at[b], normed_sem.at[b]))
+        stores[-2].start()
+        stores[-1].start()
+    for store in stores:
+        store.wait()
 
 
 def with_kernel(out_gate, key_proj, value_proj, long_filter, skip_gain, residual, norm_gain):
@@ -317,21 +318,26 @@
     anywhere = pl.BlockSpec(memory_space=pl.ANY)
     local = pl.BlockSpec(memory_space=pltpu.VMEM)
     dma = pltpu.SemaphoreType.DMA
-    mixed, normed = pl.pallas_call(
+    total, scale, columns = pl.pallas_call(
         fused,
-        out_shape=(jax.ShapeDtypeStruct(shape, bf16), jax.ShapeDtypeStruct(shape, bf16)),
-        in_specs=[anywhere] * 5 + [local] * 4,
-        out_specs=(local, local),
+        out_shape=(pltpu.VMEM(shape, f32), pltpu.VMEM((1, width), f32), pltpu.VMEM(shape, f32)),
+        in_specs=[anywhere] * 9,
+        out_specs=(local, local, local),
         scratch_shapes=[
-            *[pltpu.VMEM(shape, bf16) for _ in range(7)],
-            *[pltpu.VMEM((blocks, rows, 2 * width), f32) for _ in range(3)],
+            pltpu.VMEM((blocks, group), f32),
+            pltpu.VMEM((blocks, group), f32),
+            pltpu.VMEM((2 * width, 2 * width), bf16),
+            pltpu.VMEM((2 * width, 2 * width), bf16),
+            *[pltpu.VMEM(shape, bf16) for _ in range(4)],
+            *[pltpu.VMEM((blocks, 2, group, width), bf16) for _ in range(2)],
+            pltpu.VMEM((blocks, 2, rows, 2 * width), f32),
+            pltpu.VMEM((blocks, rows, 2 * width), f32),
             pltpu.VMEM(shape, bf16),
             pltpu.VMEM(shape, bf16),
-            pltpu.VMEM(shape, f32),
             pltpu.VMEM((lanes, 8, width), f32),
-            dma((5,)),
-            dma((2, CHUNKS, blocks)),
-            dma((2, CHUNKS, blocks)),
+            dma((9,)),
+            dma((CHUNKS, blocks)),
+            dma((CHUNKS, blocks)),
             dma((CHUNKS, blocks)),
             dma((CHUNKS, blocks)),
             dma((lanes,)),
@@ -349,6 +355,22 @@
         jnp.asarray(forward),
         jnp.asarray(inverse),
     )
+    mixed, normed = pl.pallas_call(
+        finish,
+        out_shape=(jax.ShapeDtypeStruct(shape, bf16), jax.ShapeDtypeStruct(shape, bf16)),
+        in_specs=[local, local, local],
+        out_specs=(anywhere, anywhere),
+        scratch_shapes=[
+            pltpu.VMEM(shape, bf16),
+            pltpu.VMEM(shape, bf16),
+            dma((blocks,)),
+            dma((blocks,)),
+        ],
+    )(
+        pltpu.with_memory_space_constraint(total, pltpu.VMEM),
+        pltpu.with_memory_space_constraint(scale, pltpu.VMEM),
+        pltpu.with_memory_space_constraint(columns, pltpu.VMEM),
+    )
     return mixed.reshape(chans, width), normed.reshape(chans, width)
 
 

time: 27.8 us -> 23.9 us (0.86)
  local copies, waits for them, and re-layouts: 2.42 us -> 0 us
  Pallas kernels: 24.6 us -> 23.1 us
    unnamed x4 -> x0, local copies, waits for them, and re-layouts: 2.42 us -> none
    pallas_call x1 -> x2, Pallas kernels: 24.6 us -> 23.1 us  [the longest x1 22.2 us: with_kernel(): pl.pallas_call(fused, out_shape=(pltpu.VMEM(shape, f32), pltpu.VMEM((1, w...]
where the time goes in v2:
time: 23.9 us; the launch traced here: 23.8 us
  Pallas kernels  23.1 us (97%)
  between operations  0.64 us (3%)
    pallas_call x1, Pallas kernels, with_kernel(): pl.pallas_call(fused, out_shape=(pltpu.VMEM(shape, f32), pltpu.VMEM((1, w...  22.2 us
    pallas_call x1, Pallas kernels, with_kernel(): pl.pallas_call(finish, out_shape=(jax.ShapeDtypeStruct(shape, bf16), jax....  0.92 us

profile of v2, /device:TPU:0, one launch (start us, length us, event | category | flops | bytes accessed | tf_op | source)
XLA Modules:
  0.0 23.8 jit_solution(13832628606414069009)
XLA Ops:
  0.6 22.2 %shard_map.104 = (f32[8,128,128]{2,1,0:T(8,128)S(1)}, f32[1,128]{1,0:T(1,128)S(1)}, f32[8,128,128]{2,1,0:T(8,128)S(1)}) custom-call(bf16[8,128,128]{2,1,0:T(8,128)(2,1)} %bitcast.9, bf16[8,128,128]{2,1,0:T(8,128)(2,1)} %bitcast.10, bf16[8,128,128]{2,1,0:T(8,128)(2,1)} %bitcast.11, bf16[8,128,128]{2,1,0:T(8,128)(2,1)} %bitcast.12, ...), custom_call_target="tpu_custom_call" | custom-call | tf_op jit(solution)/shard_map/pallas_call | solution.py:321
  22.8 0.9 %shard_map.105 = (bf16[8,128,128]{2,1,0:T(8,128)(2,1)}, bf16[8,128,128]{2,1,0:T(8,128)(2,1)}) custom-call(f32[8,128,128]{2,1,0:T(8,128)S(1)} %get-tuple-element.7.total_ref, f32[1,128]{1,0:T(1,128)S(1)} %get-tuple-element.8.scale_ref, f32[8,128,128]{2,1,0:T(8,128)S(1)} %get-tuple-element.9.columns_ref), custom_call_target="tpu_custom_call" | custom-call | tf_op jit(solution)/shard_map/pallas_call | solution.py:358

commit v3 on v2

--- a/solution.py
+++ b/solution.py
@@ -103,7 +103,9 @@
     return (total.astype(jnp.bfloat16), normed.astype(jnp.bfloat16))
 
 
-CHUNKS = 2
+PARTS = (5, 3)
+CHUNKS = len(PARTS)
+WHOLE = sum(PARTS)
 
 
 def spectral_tables(width):
@@ -134,7 +136,8 @@
     me = lax.axis_index("seq")
     lane = lax.axis_index("ch")
     lanes = squares_v.shape[0]
-    rows = group // CHUNKS
+    heights = [group * part // WHOLE for part in PARTS]
+    firsts = [sum(heights[:i]) for i in range(CHUNKS)]
 
     barrier = pltpu.get_barrier_semaphore()
     for step in range(1, lanes):
@@ -157,9 +160,19 @@
     pair_out[:, 1] = (key_v[...].astype(jnp.float32) * value_v[...].astype(jnp.float32)).astype(jnp.bfloat16)
     pl.semaphore_wait(barrier, blocks - 1 + lanes - 1)
 
+    def partner(step):
+        peer, bit = me, 1
+        while bit <= step:
+            if step & bit:
+                peer = peer + bit - 2 * bit * lax.rem(me // bit, 2)
+            bit *= 2
+        return peer
+
+    order = sorted(range(1, blocks), key=lambda step: (-(step // 2).bit_count(), -step))
+
     def outbound(chunk, step):
-        peer = lax.rem(me + step, blocks)
-        span = pl.ds(chunk * rows, rows)
+        peer = partner(step)
+        span = pl.ds(firsts[chunk], heights[chunk])
         return pltpu.make_async_remote_copy(
             src_ref=pair_out.at[peer, :, span],
             dst_ref=pair_in.at[me, :, span],
@@ -169,8 +182,8 @@
         )
 
     def inbound(chunk, step):
-        origin = lax.rem(me + blocks - step, blocks)
-        span = pl.ds(chunk * rows, rows)
+        origin = partner(step)
+        span = pl.ds(firsts[chunk], heights[chunk])
         return pltpu.make_async_remote_copy(
             src_ref=pair_in.at[origin, :, span],
             dst_ref=pair_in.at[origin, :, span],
@@ -180,8 +193,8 @@
         )
 
     def returning(chunk, step):
-        peer = lax.rem(me + step, blocks)
-        span = pl.ds(chunk * rows, rows)
+        peer = partner(step)
+        span = pl.ds(firsts[chunk], heights[chunk])
         return pltpu.make_async_remote_copy(
             src_ref=back_out.at[peer, span],
             dst_ref=back_in.at[me, span],
@@ -191,8 +204,8 @@
         )
 
     def returned(chunk, step):
-        origin = lax.rem(me + blocks - step, blocks)
-        span = pl.ds(chunk * rows, rows)
+        origin = partner(step)
+        span = pl.ds(firsts[chunk], heights[chunk])
         return pltpu.make_async_remote_copy(
             src_ref=back_in.at[origin, span],
             dst_ref=back_in.at[origin, span],
@@ -202,7 +215,7 @@
         )
 
     for chunk in range(CHUNKS):
-        for step in range(1, blocks):
+        for step in order:
             outbound(chunk, step).start()
 
     pair_in[me] = pair_out[me]
@@ -218,10 +231,11 @@
     sign = (1 - 2 * (lax.broadcasted_iota(jnp.int32, (8, width), 1) % 2)).astype(jnp.float32)
 
     for chunk in range(CHUNKS):
-        for step in range(1, blocks):
+        first, rows = firsts[chunk], heights[chunk]
+        for step in order:
             inbound(chunk, step).wait_recv()
-        part = pair_in[:, :, chunk * rows : (chunk + 1) * rows, :].reshape(blocks * 2 * rows, width)
-        spec[...] = jnp.dot(
+        part = pair_in[:, :, first : first + rows, :].reshape(blocks * 2 * rows, width)
+        spec[:, :, :rows] = jnp.dot(
             jnp.concatenate([part, part], axis=1), forward_ref[...], preferred_element_type=jnp.float32
         ).reshape(blocks, 2, rows, 2 * width)
 
@@ -247,26 +261,27 @@
 
         lax.fori_loop(0, rows // 8, one_octet, 0)
         timeline = jnp.dot(
-            joint[...].reshape(blocks * rows, 2 * width).astype(jnp.bfloat16),
+            joint[:, :rows].reshape(blocks * rows, 2 * width).astype(jnp.bfloat16),
             inverse_ref[...],
             preferred_element_type=jnp.float32,
         )
         timeline = (timeline[:, :width] + timeline[:, width:]).astype(jnp.bfloat16)
-        back_out[:, chunk * rows : (chunk + 1) * rows, :] = timeline.reshape(blocks, rows, width)
-        for step in range(1, blocks):
+        back_out[:, first : first + rows, :] = timeline.reshape(blocks, rows, width)
+        for step in order:
             returning(chunk, step).start()
     back_in[me] = back_out[me]
 
     squares = jnp.zeros((8, width), jnp.float32)
     for chunk in range(CHUNKS):
-        for step in range(1, blocks):
-            returned(chunk, step).wait_recv()
-        for b in range(blocks):
-            span = pl.ds(chunk * rows, rows)
+        for step in [0] + order[::-1]:
+            if step:
+                returned(chunk, step).wait_recv()
+            b = partner(step)
+            span = pl.ds(firsts[chunk], heights[chunk])
             total = total_v[b, span] + gate_v[b, span].astype(jnp.float32) * back_in[b, span].astype(jnp.float32)
             total_v[b, span] = total
-            squares = squares + jnp.sum((total * total).reshape(rows // 8, 8, width), axis=0)
-    squares_v[lane] = squares
+            squares = squares + jnp.sum((total * total).reshape(heights[chunk] // 8, 8, width), axis=0)
+    squares_v[lane] = jnp.sum(squares, axis=0, keepdims=True)
 
     def share(step, other):
         return pltpu.make_async_remote_copy(
@@ -282,11 +297,11 @@
     for step in range(1, lanes):
         origin = lax.rem(lane + lanes - step, lanes)
         share(step, (origin, origin)).wait_recv()
-    everyone = jnp.sum(jnp.sum(squares_v[...], axis=0), axis=0, keepdims=True)
+    everyone = jnp.sum(squares_v[...], axis=0)
     scale_ref[...] = lax.rsqrt(everyone / (lanes * blocks * group) + 1e-06)
 
     for chunk in range(CHUNKS):
-        for step in range(1, blocks):
+        for step in order:
             outbound(chunk, step).wait_send()
             returning(chunk, step).wait_send()
     for step in range(1, lanes):
@@ -311,7 +326,7 @@
     chans, width = key_proj.shape
     blocks, lanes = lax.axis_size("seq"), lax.axis_size("ch")
     group = chans // blocks
-    rows = group // CHUNKS
+    rows = group * max(PARTS) // WHOLE
     shape = (blocks, group, width)
     forward, inverse = spectral_tables(width)
     bf16, f32 = jnp.bfloat16, jnp.float32
@@ -334,7 +349,7 @@
             pltpu.VMEM((blocks, rows, 2 * width), f32),
             pltpu.VMEM(shape, bf16),
             pltpu.VMEM(shape, bf16),
-            pltpu.VMEM((lanes, 8, width), f32),
+            pltpu.VMEM((lanes, 1, width), f32),
             dma((9,)),
             dma((CHUNKS, blocks)),
             dma((CHUNKS, blocks)),
@@ -377,7 +392,7 @@
 def choose(out_gate, key_proj, *rest):
     chans, width = key_proj.shape
     blocks = lax.axis_size("seq")
-    tiled = chans % (blocks * CHUNKS * 16) == 0 and width % 128 == 0 and blocks <= 16
+    tiled = blocks & (blocks - 1) == 0 and chans % (blocks * WHOLE * 16) == 0 and width % 128 == 0 and blocks <= 16
     return (with_kernel if tiled else on_device)(out_gate, key_proj, *rest)
 
 

time: 23.9 us -> 23.6 us (0.987)
  Pallas kernels: 23.1 us -> 22.8 us
    pallas_call x1, Pallas kernels: 22.2 us -> 21.9 us  [with_kernel(): pl.pallas_call(fused, out_shape=(pltpu.VMEM(shape, f32), pltpu.VMEM((1, w...]
where the time goes in v3:
time: 23.6 us; the launch traced here: 23.5 us
  Pallas kernels  22.8 us (97%)
  between operations  0.64 us (3%)
    pallas_call x1, Pallas kernels, with_kernel(): pl.pallas_call(fused, out_shape=(pltpu.VMEM(shape, f32), pltpu.VMEM((1, w...  21.9 us
    pallas_call x1, Pallas kernels, with_kernel(): pl.pallas_call(finish, out_shape=(jax.ShapeDtypeStruct(shape, bf16), jax....  0.92 us

profile of v3, /device:TPU:0, one launch (start us, length us, event | category | flops | bytes accessed | tf_op | source)
XLA Modules:
  0.0 23.5 jit_solution(6985620011064815525)
XLA Ops:
  0.6 21.9 %shard_map.104 = (f32[8,128,128]{2,1,0:T(8,128)S(1)}, f32[1,128]{1,0:T(1,128)S(1)}, f32[8,128,128]{2,1,0:T(8,128)S(1)}) custom-call(bf16[8,128,128]{2,1,0:T(8,128)(2,1)} %bitcast.9, bf16[8,128,128]{2,1,0:T(8,128)(2,1)} %bitcast.10, bf16[8,128,128]{2,1,0:T(8,128)(2,1)} %bitcast.11, bf16[8,128,128]{2,1,0:T(8,128)(2,1)} %bitcast.12, ...), custom_call_target="tpu_custom_call" | custom-call | tf_op jit(solution)/shard_map/pallas_call | solution.py:336
  22.6 0.9 %shard_map.105 = (bf16[8,128,128]{2,1,0:T(8,128)(2,1)}, bf16[8,128,128]{2,1,0:T(8,128)(2,1)}) custom-call(f32[8,128,128]{2,1,0:T(8,128)S(1)} %get-tuple-element.7.total_ref, f32[1,128]{1,0:T(1,128)S(1)} %get-tuple-element.8.scale_ref, f32[8,128,128]{2,1,0:T(8,128)S(1)} %get-tuple-element.9.columns_ref), custom_call_target="tpu_custom_call" | custom-call | tf_op jit(solution)/shard_map/pallas_call | solution.py:373

commit v4 on v3

--- a/solution.py
+++ b/solution.py
@@ -311,13 +311,16 @@
 def finish(total_ref, scale_ref, columns_ref, mixed_hbm, normed_hbm, mixed_v, normed_v, mixed_sem, normed_sem):
     blocks = total_ref.shape[0]
     stores = []
+    half = blocks // 2
     for b in range(blocks):
         mixed_v[b] = total_ref[b].astype(jnp.bfloat16)
         normed_v[b] = (total_ref[b] * scale_ref[...] * columns_ref[b]).astype(jnp.bfloat16)
-        stores.append(pltpu.make_async_copy(mixed_v.at[b], mixed_hbm.at[b], mixed_sem.at[b]))
-        stores.append(pltpu.make_async_copy(normed_v.at[b], normed_hbm.at[b], normed_sem.at[b]))
-        stores[-2].start()
-        stores[-1].start()
+        if (b + 1) % half == 0:
+            part = pl.ds(b + 1 - half, half)
+            stores.append(pltpu.make_async_copy(mixed_v.at[part], mixed_hbm.at[part], mixed_sem.at[b]))
+            stores.append(pltpu.make_async_copy(normed_v.at[part], normed_hbm.at[part], normed_sem.at[b]))
+            stores[-2].start()
+            stores[-1].start()
     for store in stores:
         store.wait()
 

time: 23.6 us -> 23.7 us (level)
  no operation moved by 1% of the time
where the time goes in v4:
time: 23.7 us; the launch traced here: 23.5 us
  Pallas kernels  22.9 us (97%)
  between operations  0.64 us (3%)
    pallas_call x1, Pallas kernels, with_kernel(): pl.pallas_call(fused, out_shape=(pltpu.VMEM(shape, f32), pltpu.VMEM((1, w...  21.9 us
    pallas_call x1, Pallas kernels, with_kernel(): pl.pallas_call(finish, out_shape=(jax.ShapeDtypeStruct(shape, bf16), jax....  0.96 us

profile of v4, /device:TPU:0, one launch (start us, length us, event | category | flops | bytes accessed | tf_op | source)
XLA Modules:
  0.0 23.5 jit_solution(15376392358145468311)
XLA Ops:
  0.6 21.9 %shard_map.104 = (f32[8,128,128]{2,1,0:T(8,128)S(1)}, f32[1,128]{1,0:T(1,128)S(1)}, f32[8,128,128]{2,1,0:T(8,128)S(1)}) custom-call(bf16[8,128,128]{2,1,0:T(8,128)(2,1)} %bitcast.9, bf16[8,128,128]{2,1,0:T(8,128)(2,1)} %bitcast.10, bf16[8,128,128]{2,1,0:T(8,128)(2,1)} %bitcast.11, bf16[8,128,128]{2,1,0:T(8,128)(2,1)} %bitcast.12, ...), custom_call_target="tpu_custom_call" | custom-call | tf_op jit(solution)/shard_map/pallas_call | solution.py:339
  22.6 1.0 %shard_map.105 = (bf16[8,128,128]{2,1,0:T(8,128)(2,1)}, bf16[8,128,128]{2,1,0:T(8,128)(2,1)}) custom-call(f32[8,128,128]{2,1,0:T(8,128)S(1)} %get-tuple-element.7.total_ref, f32[1,128]{1,0:T(1,128)S(1)} %get-tuple-element.8.scale_ref, f32[8,128,128]{2,1,0:T(8,128)S(1)} %get-tuple-element.9.columns_ref), custom_call_target="tpu_custom_call" | custom-call | tf_op jit(solution)/shard_map/pallas_call | solution.py:376
